TPU v7x, 512 devices: a whole 4x4x16 slice. The times are simulated.
512 devices in a mesh: kz: 16 (over x, y_hi, core), en: 32 (over y_lo, z).
Axes of the slice: x: 4, y: 4 (y_hi: 2, y_lo: 2; y = y_hi * 2 + y_lo), z: 16, core: 2. Of those that a mesh axis runs over, the one named last changes fastest.
Arguments:
- green: bfloat16 [32, 2, 144, 4096], P('kz', None, None, 'en'), may hold values from -6 to 6
- coupling: bfloat16 [32, 82944], replicated, may hold values from -0.03125 to 0.03125
- kdiff: int32 [32, 32], replicated, may hold values from 0 to 31, each once within a row
- shift: int32 [32], replicated, may hold values from 1 to 8, as said below
- emit_weight: float32 [32], replicated, may hold values from 0.3 to 3
- absorb_weight: float32 [32], replicated, may hold values from 0.3 to 3
- neighbours: int32 [16, 4], replicated, may hold values from 0 to 15
Outputs:
- sigma: float32 [32, 2, 144, 4096], P('kz', None, None, 'en')
Inputs may be any that keep to these rules, and one draw needn't show every extreme that they name: `kdiff`: every row names each momentum point once. `shift`: some entry equals 8.
All inputs are finite; a program needn't handle non-finite values.
Results may differ from a plain program's by a relative error of at most 0.0029.
Values may be sent and summed in bfloat16 or wider, within the bound.
A program may use at most 128 MiB of HBM per device.

v0:
```python
import jax
import jax.numpy as jnp
from jax import lax
from jax.sharding import PartitionSpec as P

HALO = 8


def extended(value, sides, width):
    for axis, dim in sides:
        peers, length = (lax.axis_size(axis), value.shape[dim])
        up = [(i, (i + 1) % peers) for i in range(peers - 1)]
        down = [(j, i) for i, j in up]
        last = lax.slice_in_dim(value, length - width, length, axis=dim)
        first = lax.slice_in_dim(value, 0, width, axis=dim)
        before = lax.ppermute(last, axis, up)
        after = lax.ppermute(first, axis, down)
        value = jnp.concatenate([before, value, after], axis=dim)
    return value


def on_device(green, coupling, kdiff, shift, emit_weight, absorb_weight, neighbours):
    atoms = neighbours.shape[0]
    cols = green.shape[3]
    blocks = green.shape[2]
    local_points = green.shape[0]
    energies = cols // atoms
    margin = HALO * atoms
    whole = lax.all_gather(green, "kz", axis=0, tiled=True)
    widened = extended(whole, (("en", 3),), margin)
    all_points = kdiff.shape[0]
    krows = lax.dynamic_slice_in_dim(kdiff, lax.axis_index("kz") * local_points, local_points, 0)
    couple_all = coupling.reshape(all_points, 4, blocks, blocks)
    phonons = jnp.arange(all_points, dtype=jnp.int32)

    def select_mix(phonon, source_point):
        steps_off = shift[phonon]
        block = lax.dynamic_index_in_dim(widened, source_point, 0, keepdims=False)
        early = lax.dynamic_slice_in_dim(block, (HALO - steps_off) * atoms, cols, 2)
        late = lax.dynamic_slice_in_dim(block, (HALO + steps_off) * atoms, cols, 2)
        mixed = emit_weight[phonon] * early.astype(jnp.float32) + absorb_weight[
            phonon
        ] * late.astype(jnp.float32)
        return mixed.astype(jnp.bfloat16)

    results = []
    for local in range(local_points):
        mixes = jax.vmap(select_mix)(phonons, krows[local])
        projected = jnp.einsum(
            "qjmn,qrnc->jrmc", couple_all, mixes, preferred_element_type=jnp.float32
        )
        projected = projected.reshape(4, 2, blocks, energies, atoms)
        total = jnp.take(projected[0], neighbours[:, 0], axis=3)
        for slot in range(1, 4):
            total = total + jnp.take(projected[slot], neighbours[:, slot], axis=3)
        results.append(total.reshape(2, blocks, cols))
    return jnp.stack(results, 0)


def solution(mesh):
    return jax.shard_map(
        on_device,
        mesh=mesh,
        in_specs=(P("kz", None, None, "en"), P(), P(), P(), P(), P(), P()),
        out_specs=P("kz", None, None, "en"),
        check_vma=False,
    )
```

profile of v0, /device:TPU:1, one launch (start us, length us, event | category | flops | bytes accessed | tf_op | source)
XLA Modules:
  0.0 363.2 jit_solution(10156546521841482820)
XLA Ops:
  6.5 0.7 all-gather.2.cloned.1.call-update
  7.3 73.6 %all-gather.2.cloned.1.call-done = bf16[32,2,144,128]{3,2,1,0:T(8,128)(2,1)} async-done(((bf16[2,2,144,128]{3,2,1,0:T(8,128)(2,1)}), bf16[32,2,144,128]{3,2,1,0:T(8,128)(2,1)}) %all-gather.2.cloned.1.call-update) | async-done | bytes 2359312 | tf_op jit(solution)/shard_map/all_gather | solution.py:29
  80.8 4.6 %collective-permute-start = (bf16[32,2,144,128]{3,2,1,0:T(8,128)(2,1)}, bf16[32,2,144,128]{3,2,1,0:T(8,128)(2,1)}, u32[]{:S(2)}, u32[]{:S(2)}) collective-permute-start(bf16[32,2,144,128]{3,2,1,0:T(8,128)(2,1)} %all-gather.2.cloned.1.call-done), channel_id=1, source_target_pairs={{0,1},{1,2},{2,3},{3,4},{4,5},{5,6},{6,7},{7,8},{8,9},{9,10},{10,1... | collective-permute-start | bytes 7077896 | tf_op jit(solution)/shard_map/ppermute | solution.py:16
  85.4 1.3 collective-permute-start.1
  86.8 1.4 gather_fusion.2
  88.1 1.4 gather_fusion.3
  89.5 1.4 gather_fusion
  90.8 18.6 %reshape.120 = bf16[32,4,144,144]{3,2,1,0:T(8,128)(2,1)} reshape(bf16[32,82944]{1,0:T(8,128)(2,1)} %param.10) | data formatting | bytes 10616832 | tf_op jit(solution)/shard_map/reshape | solution.py:33
  109.5 25.1 %collective-permute-done = bf16[32,2,144,128]{3,2,1,0:T(8,128)(2,1)} collective-permute-done((bf16[32,2,144,128]{3,2,1,0:T(8,128)(2,1)}, bf16[32,2,144,128]{3,2,1,0:T(8,128)(2,1)}, u32[]{:S(2)}, u32[]{:S(2)}) %collective-permute-start) | collective-permute-done | bytes 2359328 | tf_op jit(solution)/shard_map/ppermute | solution.py:16
  134.6 3.4 constant_dynamic-update-slice_fusion.2
  138.0 1.6 constant_dynamic-update-slice_fusion.1
  139.6 0.3 collective-permute-done.1
  139.9 3.4 constant_dynamic-update-slice_fusion
  143.3 7.5 %gather_fusion.1 = bf16[32,2,144,384]{3,2,1,0:T(8,128)(2,1)} fusion(bf16[32,2,144,384]{3,2,1,0:T(8,128)(2,1)} %constant_dynamic-update-slice_fusion, s32[32]{0:T(128)S(1)} %get-tuple-element.32), kind=kCustom, calls=%fused_computation.9 | custom fusion | bytes 14156288 | tf_op jit(solution)/shard_map/vmap(jit(dynamic_index_in_dim))/gather | solution.py:38
  150.8 30.6 %copy.70 = bf16[32,2,144,384]{2,1,0,3:T(2,128)(2,1)} copy(bf16[32,2,144,384]{3,2,1,0:T(8,128)(2,1)} %gather_fusion.1) | data formatting | bytes 14155776 | tf_op jit(solution)/shard_map/vmap(jit(dynamic_index_in_dim))/gather | solution.py:38
  181.4 17.0 %gather_fusion.5 = bf16[32,2,144,128]{2,1,3,0:T(2,128)(2,1)} fusion(bf16[32,2,144,384]{2,1,0,3:T(2,128)(2,1)} %copy.70, s32[32]{0:T(128)S(1)} %get-tuple-element.34), kind=kCustom, calls=%fused_computation.13 | custom fusion | bytes 4719104 | tf_op jit(solution)/shard_map/vmap()/gather | solution.py:39
  198.3 17.0 %gather_fusion.6 = bf16[32,2,144,128]{2,1,3,0:T(2,128)(2,1)} fusion(bf16[32,2,144,384]{2,1,0,3:T(2,128)(2,1)} %copy.70, s32[32]{0:T(128)S(1)} %get-tuple-element.35), kind=kCustom, calls=%fused_computation.14 | custom fusion | bytes 4719104 | tf_op jit(solution)/shard_map/vmap()/gather | solution.py:40
  215.3 7.5 %gather_fusion.4 = bf16[32,2,144,384]{3,2,1,0:T(8,128)(2,1)} fusion(bf16[32,2,144,384]{3,2,1,0:T(8,128)(2,1)} %constant_dynamic-update-slice_fusion, s32[32]{0:T(128)S(1)} %get-tuple-element.33), kind=kCustom, calls=%fused_computation.12 | custom fusion | bytes 14156288 | tf_op jit(solution)/shard_map/vmap(jit(dynamic_index_in_dim))/gather | solution.py:38
  222.8 30.6 %copy.85 = bf16[32,2,144,384]{2,1,0,3:T(2,128)(2,1)} copy(bf16[32,2,144,384]{3,2,1,0:T(8,128)(2,1)} %gather_fusion.4) | data formatting | bytes 14155776 | tf_op jit(solution)/shard_map/vmap(jit(dynamic_index_in_dim))/gather | solution.py:38
  253.4 17.0 %gather_fusion.7 = bf16[32,2,144,128]{2,1,3,0:T(2,128)(2,1)} fusion(bf16[32,2,144,384]{2,1,0,3:T(2,128)(2,1)} %copy.85, s32[32]{0:T(128)S(1)} %get-tuple-element.34), kind=kCustom, calls=%fused_computation.15 | custom fusion | bytes 4719104 | tf_op jit(solution)/shard_map/vmap()/gather | solution.py:39
  270.4 17.0 %gather_fusion.8 = bf16[32,2,144,128]{2,1,3,0:T(2,128)(2,1)} fusion(bf16[32,2,144,384]{2,1,0,3:T(2,128)(2,1)} %copy.85, s32[32]{0:T(128)S(1)} %get-tuple-element.35), kind=kCustom, calls=%fused_computation.16 | custom fusion | bytes 4719104 | tf_op jit(solution)/shard_map/vmap()/gather | solution.py:40
  287.5 9.3 %copy.71 = bf16[32,2,144,128]{3,2,1,0:T(8,128)(2,1)S(1)} copy(bf16[32,2,144,128]{2,1,3,0:T(2,128)(2,1)} %gather_fusion.5) | data formatting | bytes 4718592 | tf_op jit(solution)/shard_map/vmap()/gather | solution.py:39
  296.8 10.6 %copy.73 = bf16[32,2,144,128]{3,2,1,0:T(8,128)(2,1)} copy(bf16[32,2,144,128]{2,1,3,0:T(2,128)(2,1)} %gather_fusion.6) | data formatting | bytes 4718592 | tf_op jit(solution)/shard_map/vmap()/gather | solution.py:40
  307.4 10.7 %copy.86 = bf16[32,2,144,128]{3,2,1,0:T(8,128)(2,1)} copy(bf16[32,2,144,128]{2,1,3,0:T(2,128)(2,1)} %gather_fusion.7) | data formatting | bytes 4718592 | tf_op jit(solution)/shard_map/vmap()/gather | solution.py:39
  318.1 10.6 %copy.88 = bf16[32,2,144,128]{3,2,1,0:T(8,128)(2,1)} copy(bf16[32,2,144,128]{2,1,3,0:T(2,128)(2,1)} %gather_fusion.8) | data formatting | bytes 4718592 | tf_op jit(solution)/shard_map/vmap()/gather | solution.py:40
  328.7 6.6 %fusion.6 = (bf16[32,2,144,128,1]{3,2,1,0,4:T(8,128)(2,1)}, bf16[32,2,144,128,1]{3,2,1,0,4:T(8,128)(2,1)S(1)}) fusion(bf16[32,2,144,128]{3,2,1,0:T(8,128)(2,1)} %copy.73, bf16[32,2,144,128]{3,2,1,0:T(8,128)(2,1)S(1)} %copy.71, f32[32]{0:T(128)S(1)} %gather_fusion.3, f32[32]{0:T(128)S(1)} %gather_fusion, bf16[32,2,144,128]{3,2,1,0:T(8,128)(2,1)} %copy.88, ...), kind=kLoop, calls=%fused_computation.25 | loop fusion | flops 14155776 | bytes 14156032 | tf_op jit(solution)/shard_map/vmap()/convert_element_type | solution.py:44
  335.3 6.0 %fusion.15 = f32[4,2,144,128]{3,2,0,1:T(8,128)S(1)} fusion(bf16[32,4,144,144]{3,2,1,0:T(8,128)(2,1)} %reshape.120, bf16[32,2,144,128,1]{3,2,1,0,4:T(8,128)(2,1)S(1)} %get-tuple-element.31), kind=kOutput, calls=%fused_computation.30 | convolution fusion | flops 1358954496 | bytes 8257536 | tf_op jit(solution)/shard_map/qjmn,qrnc->jrmc/dot_general | solution.py:49
  341.5 0.2 copy.92
  341.8 0.2 copy.94
  342.1 0.2 copy.96
  342.4 0.2 copy.98
  342.6 6.4 %fusion.10 = f32[4,2,144,128]{3,2,0,1:T(8,128)S(1)} fusion(bf16[32,4,144,144]{3,2,1,0:T(8,128)(2,1)} %reshape.120, bf16[32,2,144,128,1]{3,2,1,0,4:T(8,128)(2,1)} %get-tuple-element.30), kind=kOutput, calls=%fused_computation.29 | convolution fusion | flops 1358954496 | bytes 8257536 | tf_op jit(solution)/shard_map/qjmn,qrnc->jrmc/dot_general | solution.py:49
  349.2 0.2 copy.77
  349.3 0.6 gather_fusion.13
  349.9 0.6 gather_fusion.9
  350.6 0.2 copy.79
  350.8 0.6 gather_fusion.14
  351.3 0.6 gather_fusion.10
  352.0 0.2 copy.81
  352.2 0.6 gather_fusion.15
  352.8 0.6 gather_fusion.11
  353.5 0.2 copy.83
  353.7 0.6 gather_fusion.16
  354.2 0.6 gather_fusion.12
  354.8 0.2 bitcast_add_fusion.3
  355.0 0.2 copy.84
  355.2 0.2 copy.99
  355.4 0.9 copy.100
  (28 shorter events, 1.2 us)
Async XLA Ops:
  6.5 102.9 %copy-start = (s32[32,32]{1,0:T(8,128)S(1)}, s32[32,32]{1,0:T(8,128)}, u32[]{:S(2)}) copy-start(s32[32,32]{1,0:T(8,128)} %param.11) | copy-start | bytes 12292
  6.5 74.3 %all-gather.2.cloned.1.call-start = ((), (), s32[]{:S(2)}) async-start(), calls=%async_computation | async-start | bytes 2506752 | tf_op jit(solution)/shard_map/all_gather | solution.py:29
  80.8 53.8 %collective-permute-start = (bf16[32,2,144,128]{3,2,1,0:T(8,128)(2,1)}, bf16[32,2,144,128]{3,2,1,0:T(8,128)(2,1)}, u32[]{:S(2)}, u32[]{:S(2)}) collective-permute-start(bf16[32,2,144,128]{3,2,1,0:T(8,128)(2,1)} %all-gather.2.cloned.1.call-done), channel_id=1, source_target_pairs={{0,1},{1,2},{2,3},{3,4},{4,5},{5,6},{6,7},{7,8},{8,9},{9,10},{10,1... | collective-permute-start | bytes 7077896 | tf_op jit(solution)/shard_map/ppermute | solution.py:16
  85.4 54.4 %collective-permute-start.1 = (bf16[32,2,144,128]{3,2,1,0:T(8,128)(2,1)}, bf16[32,2,144,128]{3,2,1,0:T(8,128)(2,1)}, u32[]{:S(2)}, u32[]{:S(2)}) collective-permute-start(bf16[32,2,144,128]{3,2,1,0:T(8,128)(2,1)} %all-gather.2.cloned.1.call-done), channel_id=1, source_target_pairs={{1,0},{2,1},{3,2},{4,3},{5,4},{6,5},{7,6},{8,7},{9,8},{10,9},{11,1... | collective-permute-start | bytes 7077896 | tf_op jit(solution)/shard_map/ppermute | solution.py:17
  90.8 18.6 %copy-start.3 = (s32[16,4]{0,1:T(4,128)S(1)}, s32[16,4]{0,1:T(4,128)}, u32[]{:S(2)}) copy-start(s32[16,4]{0,1:T(4,128)} %param.15) | copy-start | bytes 772
  109.4 28.6 %copy-start.2 = (bf16[32,2,144,128]{3,2,1,0:T(8,128)(2,1)S(1)}, bf16[32,2,144,128]{3,2,1,0:T(8,128)(2,1)}, u32[]{:S(2)}) copy-start(bf16[32,2,144,128]{3,2,1,0:T(8,128)(2,1)} %all-gather.2.cloned.1.call-done) | copy-start | bytes 7077892
  353.6 2.7 copy-start.1
Sparse Core Ops, SparseCore 0:
  10.6 70.1 all-gather.1
where the time goes:
time: 369 us; the launch traced here: 363 us
  local copies, waits for them, and re-layouts  225 us (61%)
  waiting for transfers between devices  99.6 us (27%)
  between operations  13.7 us (4%)
  matrix products  12.4 us (3%)
  other arithmetic  6.9 us (2%)
  starting transfers between devices  5.91 us (2%)
    gather x4, local copies, waits for them, and re-layouts, select_mix(): block = lax.dynamic_index_in_dim(widened, source_point, 0, keepdims=False)  76.1 us
    all_gather x1, waiting for transfers between devices, on_device(): whole = lax.all_gather(green, 'kz', axis=0, tiled=True)  73.6 us
    gather x4, local copies, waits for them, and re-layouts, select_mix(): late = lax.dynamic_slice_in_dim(block, (HALO + steps_off) * atoms, cols, 2)  55.3 us
    gather x4, local copies, waits for them, and re-layouts, select_mix(): early = lax.dynamic_slice_in_dim(block, (HALO - steps_off) * atoms, cols, 2)  53.9 us
    ppermute x1, waiting for transfers between devices, extended(): before = lax.ppermute(last, axis, up)  25.1 us
    reshape x1, local copies, waits for them, and re-layouts, on_device(): couple_all = coupling.reshape(all_points, 4, blocks, blocks)  18.6 us
    dot_general x2, matrix products, on_device(): jnp.einsum('qjmn,qrnc->jrmc', couple_all, mixes, preferred_element_type=j...  12.4 us
  transfers between devices with their start and end apart: 3, of which 3 were waited for; matrix products, arithmetic and copies ran while one was open for 8% of the time, Pallas kernels for 0%

commit v1 on v0

v1 whole, which is shorter than its diff:
```python
import jax
import jax.numpy as jnp
from jax import lax
from jax.experimental import pallas as pl
from jax.experimental.pallas import tpu as pltpu
from jax.sharding import PartitionSpec as P

BLK = 144
LANES = 128
NA = 16
NK = 32
SPAN = 16 * BLK
DEPTH = 8 * BLK
MESH = pl.DeviceIdType.MESH
BF16 = jnp.bfloat16
F32 = jnp.float32


def relay_couple(cbuf, cmain, ctail, head, tail, spread, j):
    @pl.loop(0, BLK // 16)
    def _(t):
        chunk = j * (BLK // 16) + t
        base = pl.multiple_of(chunk * SPAN, LANES)
        row = pl.multiple_of(chunk * 16, 16)
        for half in range(NK // 16):
            x = cbuf[16 * half : 16 * half + 16, pl.ds(base, SPAN)]
            for m in range(16):
                o = m * BLK
                a = x[:, o : o + LANES].astype(F32)
                b = x[:, o + LANES : o + BLK].astype(F32)
                for u in range(2):
                    r0 = ((2 * half + u) * 16 + m) * 8
                    head[r0 : r0 + 8, :] = a[8 * u : 8 * u + 8]
                    tail[r0 : r0 + 8, 0:16] = b[8 * u : 8 * u + 8]
            ends = []
            for u in range(2):
                for v in range(8):
                    q = 16 * half + 8 * u + v
                    rows = pl.ds((2 * half + u) * 128 + v, 16, stride=8)
                    cmain[q, pl.ds(row, 16), :] = head[rows, :].astype(BF16)
                    ends.append(tail[rows, :].astype(BF16))
            wide = jnp.dot(jnp.concatenate(ends, 0), spread, preferred_element_type=F32)
            for v in range(16):
                ctail[16 * half + v, pl.ds(row, 16), :] = wide[16 * v : 16 * v + 16].astype(BF16)


def shift_tables(table, before, own, after):
    for s in range(1, 8):
        w = NA * s
        table[s] = jnp.concatenate([before[:, LANES - w :], own[:, : LANES - w]], 1)
        table[8 + s] = jnp.concatenate([own[:, w:], after[:, :w]], 1)
    table[0] = before
    table[8] = after


def invert(kd, first):
    lane = lax.broadcasted_iota(jnp.int32, (NK, NK), 1)
    wide = lax.broadcasted_iota(jnp.int32, (NK, LANES), 1)
    result = jnp.zeros((NK, LANES), jnp.int32)
    for i in range(8):
        q = jnp.sum(jnp.where(kd == first + i, lane, 0), axis=1, keepdims=True)
        result = jnp.where(wide == i, jnp.minimum(q, NK - 1), result)
    return result


def sources(nbr, j):
    lane = lax.broadcasted_iota(jnp.int32, (8, LANES), 1)
    atom = lane % NA
    source = lane - atom
    for a in range(NA):
        source = jnp.where(atom == a, source + nbr[j, a], source)
    return source


def kernel(
    green, couple, kdiff, shift_in, emit_in, absorb_in, nbr_in, out,
    own, cbuf, cmain, ctail, head, tail, got, tab, rhs, mine, sendbuf, recvbuf, lanes_from, proj,
    kd, invv, inv, shift, emit, absorb, nbr,
    csem, lsem, gs, gr, rs, rr,
):
    kz, en = lax.axis_index("kz"), lax.axis_index("en")
    count = lax.axis_size("en")
    x, g = kz // 4, kz % 4
    h, c = g // 2, g % 2
    partner = (kz + 1 - 2 * c, en)
    across = (kz + 2 - 4 * h, en)
    later = (kz, (en + 1) % count)
    earlier = (kz, (en + count - 1) % count)

    def column(d):
        return ((kz + 4 * d) % 16, en)

    def fetch(j):
        cols = pl.ds(j * BLK * BLK, BLK * BLK)
        return pltpu.make_async_copy(couple.at[:, cols], cbuf.at[:, cols], csem.at[j])

    barrier = pltpu.get_barrier_semaphore()
    for peer in (partner, across, later, earlier, column(1), column(2), column(3)):
        pl.semaphore_signal(barrier, inc=1, device_id=peer, device_id_type=MESH)
    loads = [
        pltpu.make_async_copy(src, dst, lsem.at[n])
        for n, (src, dst) in enumerate(
            ((kdiff, kd), (shift_in, shift), (emit_in, emit), (absorb_in, absorb), (nbr_in, nbr), (green, own))
        )
    ]
    for load in loads:
        load.start()
    for j in range(4):
        fetch(j).start()
    tail[...] = jnp.zeros_like(tail)
    pl.semaphore_wait(barrier, 7)

    def hop(n, src, dst, peer):
        return pltpu.make_async_remote_copy(
            src_ref=src, dst_ref=dst, send_sem=gs.at[n], recv_sem=gr.at[n],
            device_id=peer, device_id_type=MESH,
        )

    hops = [
        hop(0, green, got.at[2, 1], across),
        hop(1, green, got.at[0, 0], later),
        hop(2, green, got.at[0, 2], earlier),
        hop(3, green, got.at[1, 1], partner),
        hop(4, got.at[2, 1], got.at[2, 0], later),
        hop(5, got.at[2, 1], got.at[2, 2], earlier),
        hop(6, got.at[2, 1], got.at[3, 1], partner),
        hop(7, got.at[0, 0], got.at[1, 0], partner),
        hop(8, got.at[0, 2], got.at[1, 2], partner),
        hop(9, got.at[2, 0], got.at[3, 0], partner),
        hop(10, got.at[2, 2], got.at[3, 2], partner),
    ]
    for n in range(4):
        hops[n].start()
    for load in loads:
        load.wait()
    invv[...] = invert(kd[...], 8 * x)
    to_scalar = pltpu.make_async_copy(invv, inv, lsem.at[0])
    to_scalar.start()
    for j in range(4):
        lanes_from[j] = sources(nbr, j)

    def tables(rho):
        @pl.loop(0, 4)
        def _(ir):
            i, r = ir // 2, ir % 2
            here = own[i, r] if rho == 0 else got[rho, 1, i, r]
            before, after = got[rho, 0, i, r], got[rho, 2, i, r]
            before = jnp.where(en > 0, before, jnp.zeros_like(before))
            after = jnp.where(en < count - 1, after, jnp.zeros_like(after))
            shift_tables(tab.at[2 * rho + i, :, r], before, here, after)

    fine = lax.broadcasted_iota(jnp.int32, (LANES, LANES), 1) % 16
    spread = jnp.where(lax.broadcasted_iota(jnp.int32, (LANES, LANES), 0) == fine, 1.0, 0.0).astype(BF16)

    def relay(j):
        fetch(j).wait()
        relay_couple(cbuf, cmain, ctail, head, tail, spread, j)

    relay(0)
    hops[0].wait_recv()
    for n in (4, 5, 6):
        hops[n].start()
    hops[1].wait_recv()
    hops[7].start()
    hops[2].wait_recv()
    hops[8].start()
    for j in range(1, 4):
        relay(j)
    hops[4].wait_recv()
    hops[9].start()
    hops[5].wait_recv()
    hops[10].start()
    tables(0)
    hops[3].wait_recv()
    hops[7].wait_recv()
    hops[8].wait_recv()
    tables(1)
    tables(2)
    hops[6].wait_recv()
    hops[9].wait_recv()
    hops[10].wait_recv()
    tables(3)
    to_scalar.wait()

    places = []
    for rho in range(4):
        owner = 2 * ((h + rho // 2) % 2) + (c + rho % 2) % 2
        for i in range(2):
            places.append(2 * owner + i)
    group = lax.broadcasted_iota(jnp.int32, (4 * BLK, LANES), 1) // 16

    def ring(dd):
        return pltpu.make_async_remote_copy(
            src_ref=sendbuf.at[dd], dst_ref=recvbuf.at[dd],
            send_sem=rs.at[dd], recv_sem=rr.at[dd],
            device_id=column(dd + 1), device_id_type=MESH,
        )

    def phonons_of(dd, kk):
        k = 8 * ((x + dd + 1) % 4) + 2 * g + kk
        return [inv[k, place] for place in places]

    def prepare(dd, kk):
        for slot, q in enumerate(phonons_of(dd, kk)):
            s = shift[q] % 8
            early = tab[slot, s].astype(F32)
            late = tab[slot, 8 + s].astype(F32)
            mix = (emit[q] * early + absorb[q] * late).astype(BF16)
            for r in range(2):
                lanes = slice(r * LANES, (r + 1) * LANES)
                rhs[kk, slot * LANES : (slot + 1) * LANES, lanes] = mix[r, :LANES]
                rhs[kk, 8 * LANES + slot * 16 : 8 * LANES + (slot + 1) * 16, lanes] = mix[r, LANES:]

    def project(dd, kk):
        phonons = phonons_of(dd, kk)
        last = ctail[phonons[0]]
        for slot in range(1, 8):
            last = jnp.where(group == slot, ctail[phonons[slot]], last)
        lhs = jnp.concatenate([cmain[q] for q in phonons] + [last], axis=1)
        proj[kk] = jnp.dot(lhs, rhs[kk], preferred_element_type=F32)

    def gather(dd):
        for kk in range(2):
            for r in range(2):
                for m in range(0, BLK, 8):
                    total = None
                    for j in range(4):
                        piece = proj[kk, j * BLK + m : j * BLK + m + 8, r * LANES : (r + 1) * LANES]
                        piece = jnp.take_along_axis(piece, lanes_from[j], axis=1, mode="promise_in_bounds")
                        total = piece if total is None else total + piece
                    mine[kk, r, m : m + 8] = total
                sendbuf[dd, kk, r] = mine[kk, r].astype(BF16)

    prepare(0, 0)
    prepare(0, 1)
    project(0, 0)
    prepare(1, 0)
    project(0, 1)

    @pl.loop(1, 4)
    def _(dd):
        gather(dd - 1)
        prepare(dd, 1)
        project(dd, 0)
        prepare(dd + 1, 0)
        project(dd, 1)
        ring(dd - 1).start()

    gather(3)
    for n in range(11):
        hops[n].wait_send()
    for dd in range(3):
        ring(dd).wait_recv()
    for kk in range(2):
        for r in range(2):
            out[kk, r] = mine[kk, r] + (
                recvbuf[0, kk, r].astype(F32)
                + recvbuf[1, kk, r].astype(F32)
                + recvbuf[2, kk, r].astype(F32)
            )
    for dd in range(3):
        ring(dd).wait_send()


def on_device(green, coupling, kdiff, shift, emit_weight, absorb_weight, neighbours):
    hbm = pl.BlockSpec(memory_space=pl.ANY)
    block = (2, 2, BLK, LANES)
    return pl.pallas_call(
        kernel,
        out_shape=jax.ShapeDtypeStruct(green.shape, F32),
        in_specs=[hbm] * 7,
        out_specs=pl.BlockSpec(memory_space=pltpu.VMEM),
        scratch_shapes=[
            pltpu.VMEM(block, BF16),
            pltpu.VMEM((NK, 4 * BLK * BLK), BF16),
            pltpu.VMEM((NK, 4 * BLK, LANES), BF16),
            pltpu.VMEM((NK, 4 * BLK, LANES), BF16),
            pltpu.VMEM((512, LANES), F32),
            pltpu.VMEM((512, LANES), F32),
            pltpu.VMEM((4, 3) + block, BF16),
            pltpu.VMEM((8, 16, 2, BLK, LANES), BF16),
            pltpu.VMEM((2, DEPTH, 2 * LANES), BF16),
            pltpu.VMEM(block, F32),
            pltpu.VMEM((4,) + block, BF16),
            pltpu.VMEM((3,) + block, BF16),
            pltpu.VMEM((4, 8, LANES), jnp.int32),
            pltpu.VMEM((2, 4 * BLK, 2 * LANES), F32),
            pltpu.VMEM((NK, NK), jnp.int32),
            pltpu.VMEM((NK, LANES), jnp.int32),
            pltpu.SMEM((NK, LANES), jnp.int32),
            pltpu.SMEM((NK,), jnp.int32),
            pltpu.SMEM((NK,), F32),
            pltpu.SMEM((NK,), F32),
            pltpu.SMEM((4, NA), jnp.int32),
            pltpu.SemaphoreType.DMA((4,)),
            pltpu.SemaphoreType.DMA((6,)),
            pltpu.SemaphoreType.DMA((11,)),
            pltpu.SemaphoreType.DMA((11,)),
            pltpu.SemaphoreType.DMA((3,)),
            pltpu.SemaphoreType.DMA((3,)),
        ],
        compiler_params=pltpu.CompilerParams(
            collective_id=0, has_side_effects=True, vmem_limit_bytes=62 * 2**20
        ),
    )(green, coupling, kdiff, shift, emit_weight, absorb_weight, neighbours.T)


def solution(mesh):
    return jax.shard_map(
        on_device,
        mesh=mesh,
        in_specs=(P("kz", None, None, "en"), P(), P(), P(), P(), P(), P()),
        out_specs=P("kz", None, None, "en"),
        check_vma=False,
    )
```

time: 369 us -> 49.3 us (0.13); the launches traced: 363 us -> 49.1 us
  local copies, waits for them, and re-layouts: 225 us -> 1.7 us
  waiting for transfers between devices: 99.6 us -> 0 us
  Pallas kernels: 0 us -> 47.4 us
  between operations: 13.7 us -> 0.01 us
  matrix products: 12.4 us -> 0 us
  other arithmetic: 6.9 us -> 0 us
  starting transfers between devices: 5.91 us -> 0 us
    gather x23 -> x0, local copies, waits for them, and re-layouts: 194 us -> none  [the longest x4 76.1 us: select_mix(): block = lax.dynamic_index_in_dim(widened, source_point, 0, keepdims=False)]
    all_gather x1 -> x0, waiting for transfers between devices: 73.6 us -> none  [on_device(): whole = lax.all_gather(green, 'kz', axis=0, tiled=True)]
    pallas_call x0 -> x1, Pallas kernels: none -> 47.4 us  [on_device(): pl.pallas_call(kernel, out_shape=jax.ShapeDtypeStruct(green.shape, F32),...]
    ppermute x2 -> x0, waiting for transfers between devices: 25.3 us -> none  [the longest x1 25.1 us: extended(): before = lax.ppermute(last, axis, up)]
    reshape x1 -> x0, local copies, waits for them, and re-layouts: 18.6 us -> none  [on_device(): couple_all = coupling.reshape(all_points, 4, blocks, blocks)]
    dot_general x2 -> x0, matrix products: 12.4 us -> none  [on_device(): jnp.einsum('qjmn,qrnc->jrmc', couple_all, mixes, preferred_element_type=j...]
    convert_element_type x1 -> x0, other arithmetic: 6.6 us -> none  [select_mix(): return mixed.astype(jnp.bfloat16)]
    ppermute x2 -> x0, starting transfers between devices: 5.9 us -> none  [the longest x1 4.62 us: extended(): before = lax.ppermute(last, axis, up)]
  transfers between devices with their start and end apart: 3 -> 0, of which waited for: 3 -> 0; matrix products, arithmetic and copies ran while one was open for 8% -> 0% of each run, Pallas kernels for 0% -> 0%
where the time goes in v1:
time: 49.3 us; the launch traced here: 49.1 us
  Pallas kernels  47.4 us (96%)
  local copies, waits for them, and re-layouts  1.7 us (3%)
    pallas_call x1, Pallas kernels, on_device(): pl.pallas_call(kernel, out_shape=jax.ShapeDtypeStruct(green.shape, F32),...  47.4 us
    unnamed x1, local copies, waits for them, and re-layouts  1.7 us

profile of v1, /device:TPU:1, one launch (start us, length us, event | category | flops | bytes accessed | tf_op | source)
XLA Modules:
  0.0 49.1 jit_solution(12358987224723208418)
XLA Ops:
  0.0 47.4 %shard_map.73 = f32[2,2,144,128]{3,2,1,0:T(8,128)} custom-call(bf16[2,2,144,128]{3,2,1,0:T(8,128)(2,1)} %green.1, bf16[32,82944]{1,0:T(8,128)(2,1)} %couple.1, s32[32,32]{1,0:T(8,128)} %kdiff.1, s32[32]{0:T(128)} %shift_in.1, f32[32]{0:T(128)} %emit_in.1, f32[32]{0:T(128)} %absorb_in.1, s32[4,16]{1,0:T(4,128)} %bitcast.1), custom_call_target="tpu_custom_call" | custom-call | tf_op jit(solution)/shard_map/pallas_call | solution.py:268
  47.5 1.7 %copy.9 = f32[2,2,144,128]{3,2,1,0:T(8,128)} copy(f32[2,2,144,128]{3,2,1,0:T(8,128)} %shard_map.73) | data formatting | bytes 589824

commit v2 on v1

--- a/solution.py
+++ b/solution.py
@@ -10,18 +10,19 @@
 NA = 16
 NK = 32
 SPAN = 16 * BLK
-DEPTH = 8 * BLK
+FOLD = 3
 MESH = pl.DeviceIdType.MESH
 BF16 = jnp.bfloat16
 F32 = jnp.float32
 
 
-def relay_couple(cbuf, cmain, ctail, head, tail, spread, j):
-    @pl.loop(0, BLK // 16)
-    def _(t):
-        chunk = j * (BLK // 16) + t
-        base = pl.multiple_of(chunk * SPAN, LANES)
-        row = pl.multiple_of(chunk * 16, 16)
+def relay_couple(cbuf, cmain, ctail, head, tail, spread, part):
+    for f in range(FOLD):
+        chunk = part * FOLD + f
+        base = chunk * SPAN
+        row = chunk * 16
+        if not isinstance(part, int):
+            base, row = pl.multiple_of(base, LANES), pl.multiple_of(row, 16)
         for half in range(NK // 16):
             x = cbuf[16 * half : 16 * half + 16, pl.ds(base, SPAN)]
             for m in range(16):
@@ -30,16 +31,16 @@
                 b = x[:, o + LANES : o + BLK].astype(F32)
                 for u in range(2):
                     r0 = ((2 * half + u) * 16 + m) * 8
-                    head[r0 : r0 + 8, :] = a[8 * u : 8 * u + 8]
-                    tail[r0 : r0 + 8, 0:16] = b[8 * u : 8 * u + 8]
-            ends = []
+                    head[f, r0 : r0 + 8, :] = a[8 * u : 8 * u + 8]
+                    tail[f, r0 : r0 + 8, 0:16] = b[8 * u : 8 * u + 8]
+            tips = []
             for u in range(2):
                 for v in range(8):
                     q = 16 * half + 8 * u + v
                     rows = pl.ds((2 * half + u) * 128 + v, 16, stride=8)
-                    cmain[q, pl.ds(row, 16), :] = head[rows, :].astype(BF16)
-                    ends.append(tail[rows, :].astype(BF16))
-            wide = jnp.dot(jnp.concatenate(ends, 0), spread, preferred_element_type=F32)
+                    cmain[q, pl.ds(row, 16), :] = head[f, rows, :].astype(BF16)
+                    tips.append(tail[f, rows, :].astype(BF16))
+            wide = jnp.dot(jnp.concatenate(tips, 0), spread, preferred_element_type=F32)
             for v in range(16):
                 ctail[16 * half + v, pl.ds(row, 16), :] = wide[16 * v : 16 * v + 16].astype(BF16)
 
@@ -74,7 +75,7 @@
 
 def kernel(
     green, couple, kdiff, shift_in, emit_in, absorb_in, nbr_in, out,
-    own, cbuf, cmain, ctail, head, tail, got, tab, rhs, mine, sendbuf, recvbuf, lanes_from, proj,
+    own, cbuf, cmain, ctail, head, tail, got, tab, rhs, ends, mine, sendbuf, recvbuf, lanes_from, proj,
     kd, invv, inv, shift, emit, absorb, nbr,
     csem, lsem, gs, gr, rs, rr,
 ):
@@ -111,10 +112,14 @@
     pl.semaphore_wait(barrier, 7)
 
     def hop(n, src, dst, peer):
-        return pltpu.make_async_remote_copy(
-            src_ref=src, dst_ref=dst, send_sem=gs.at[n], recv_sem=gr.at[n],
-            device_id=peer, device_id_type=MESH,
-        )
+        return [
+            pltpu.make_async_remote_copy(
+                src_ref=src.at[i], dst_ref=dst.at[i],
+                send_sem=gs.at[2 * n + i], recv_sem=gr.at[2 * n + i],
+                device_id=peer, device_id_type=MESH,
+            )
+            for i in range(2)
+        ]
 
     hops = [
         hop(0, green, got.at[2, 1], across),
@@ -129,8 +134,15 @@
         hop(9, got.at[2, 0], got.at[3, 0], partner),
         hop(10, got.at[2, 2], got.at[3, 2], partner),
     ]
-    for n in range(4):
-        hops[n].start()
+
+    def forward(n, onward, i):
+        hops[n][i].wait_recv()
+        for target in onward:
+            hops[target][i].start()
+
+    for i in range(2):
+        for n in range(4):
+            hops[n][i].start()
     for load in loads:
         load.wait()
     invv[...] = invert(kd[...], 8 * x)
@@ -139,47 +151,50 @@
     for j in range(4):
         lanes_from[j] = sources(nbr, j)
 
+    def table(rho, ir):
+        i, r = ir // 2, ir % 2
+        here = own[i, r] if rho == 0 else got[rho, 1, i, r]
+        before, after = got[rho, 0, i, r], got[rho, 2, i, r]
+        before = jnp.where(en > 0, before, jnp.zeros_like(before))
+        after = jnp.where(en < count - 1, after, jnp.zeros_like(after))
+        shift_tables(tab.at[2 * rho + i, :, r], before, here, after)
+
     def tables(rho):
         @pl.loop(0, 4)
         def _(ir):
-            i, r = ir // 2, ir % 2
-            here = own[i, r] if rho == 0 else got[rho, 1, i, r]
-            before, after = got[rho, 0, i, r], got[rho, 2, i, r]
-            before = jnp.where(en > 0, before, jnp.zeros_like(before))
-            after = jnp.where(en < count - 1, after, jnp.zeros_like(after))
-            shift_tables(tab.at[2 * rho + i, :, r], before, here, after)
+            table(rho, ir)
 
     fine = lax.broadcasted_iota(jnp.int32, (LANES, LANES), 1) % 16
     spread = jnp.where(lax.broadcasted_iota(jnp.int32, (LANES, LANES), 0) == fine, 1.0, 0.0).astype(BF16)
 
-    def relay(j):
-        fetch(j).wait()
-        relay_couple(cbuf, cmain, ctail, head, tail, spread, j)
-
-    relay(0)
-    hops[0].wait_recv()
-    for n in (4, 5, 6):
-        hops[n].start()
-    hops[1].wait_recv()
-    hops[7].start()
-    hops[2].wait_recv()
-    hops[8].start()
-    for j in range(1, 4):
-        relay(j)
-    hops[4].wait_recv()
-    hops[9].start()
-    hops[5].wait_recv()
-    hops[10].start()
+    def relay(first, last):
+        for j in range(4):
+            if first <= j * 36 // (4 * FOLD) < last:
+                fetch(j).wait()
+
+        @pl.loop(first, last)
+        def _(part):
+            relay_couple(cbuf, cmain, ctail, head, tail, spread, part)
+
+    relay(0, 4)
+    forward(0, (4, 5, 6), 0)
+    relay(4, 6)
+    forward(1, (7,), 0)
+    forward(2, (8,), 0)
+    forward(0, (4, 5, 6), 1)
+    relay(6, 8)
+    forward(1, (7,), 1)
+    forward(2, (8,), 1)
+    relay(8, 12)
+    forward(4, (9,), 0)
+    forward(5, (10,), 0)
     tables(0)
-    hops[3].wait_recv()
-    hops[7].wait_recv()
-    hops[8].wait_recv()
+    forward(4, (9,), 1)
+    forward(5, (10,), 1)
+    for n in (3, 7, 8):
+        for i in range(2):
+            forward(n, (), i)
     tables(1)
-    tables(2)
-    hops[6].wait_recv()
-    hops[9].wait_recv()
-    hops[10].wait_recv()
-    tables(3)
     to_scalar.wait()
 
     places = []
@@ -200,24 +215,31 @@
         k = 8 * ((x + dd + 1) % 4) + 2 * g + kk
         return [inv[k, place] for place in places]
 
-    def prepare(dd, kk):
+    def prepare(dd, kk, half):
         for slot, q in enumerate(phonons_of(dd, kk)):
+            if slot // 4 != half:
+                continue
             s = shift[q] % 8
             early = tab[slot, s].astype(F32)
             late = tab[slot, 8 + s].astype(F32)
             mix = (emit[q] * early + absorb[q] * late).astype(BF16)
             for r in range(2):
                 lanes = slice(r * LANES, (r + 1) * LANES)
-                rhs[kk, slot * LANES : (slot + 1) * LANES, lanes] = mix[r, :LANES]
-                rhs[kk, 8 * LANES + slot * 16 : 8 * LANES + (slot + 1) * 16, lanes] = mix[r, LANES:]
-
-    def project(dd, kk):
+                rhs[kk, slot % 4 * LANES : (slot % 4 + 1) * LANES, lanes] = mix[r, :LANES]
+                ends[dd % 4, kk, slot * 16 : (slot + 1) * 16, lanes] = mix[r, LANES:]
+
+    def project(dd, kk, half):
         phonons = phonons_of(dd, kk)
+        lhs = jnp.concatenate([cmain[q] for q in phonons[4 * half : 4 * half + 4]], axis=1)
+        part = jnp.dot(lhs, rhs[kk], preferred_element_type=F32)
+        if half == 0:
+            proj[dd, kk] = part
+            return
         last = ctail[phonons[0]]
         for slot in range(1, 8):
             last = jnp.where(group == slot, ctail[phonons[slot]], last)
-        lhs = jnp.concatenate([cmain[q] for q in phonons] + [last], axis=1)
-        proj[kk] = jnp.dot(lhs, rhs[kk], preferred_element_type=F32)
+        part = part + jnp.dot(last, ends[dd, kk], preferred_element_type=F32)
+        proj[dd, kk] = proj[dd, kk] + part
 
     def gather(dd):
         for kk in range(2):
@@ -225,30 +247,45 @@
                 for m in range(0, BLK, 8):
                     total = None
                     for j in range(4):
-                        piece = proj[kk, j * BLK + m : j * BLK + m + 8, r * LANES : (r + 1) * LANES]
+                        piece = proj[dd, kk, j * BLK + m : j * BLK + m + 8, r * LANES : (r + 1) * LANES]
                         piece = jnp.take_along_axis(piece, lanes_from[j], axis=1, mode="promise_in_bounds")
                         total = piece if total is None else total + piece
                     mine[kk, r, m : m + 8] = total
                 sendbuf[dd, kk, r] = mine[kk, r].astype(BF16)
 
-    prepare(0, 0)
-    prepare(0, 1)
-    project(0, 0)
-    prepare(1, 0)
-    project(0, 1)
+    prepare(0, 0, 0)
+
+    @pl.loop(0, 4)
+    def _(dd):
+        prepare(dd, 1, 0)
+        project(dd, 0, 0)
+        table(2, dd)
+        prepare(dd + 1, 0, 0)
+        project(dd, 1, 0)
+
+    for n in (6, 9, 10):
+        for i in range(2):
+            forward(n, (), i)
+    tables(3)
+    prepare(0, 0, 1)
+    prepare(0, 1, 1)
+    project(0, 0, 1)
+    prepare(1, 0, 1)
+    project(0, 1, 1)
 
     @pl.loop(1, 4)
     def _(dd):
         gather(dd - 1)
-        prepare(dd, 1)
-        project(dd, 0)
-        prepare(dd + 1, 0)
-        project(dd, 1)
+        prepare(dd, 1, 1)
+        project(dd, 0, 1)
+        prepare(dd + 1, 0, 1)
+        project(dd, 1, 1)
         ring(dd - 1).start()
 
     gather(3)
-    for n in range(11):
-        hops[n].wait_send()
+    for pair in hops:
+        for piece in pair:
+            piece.wait_send()
     for dd in range(3):
         ring(dd).wait_recv()
     for kk in range(2):
@@ -275,16 +312,17 @@
             pltpu.VMEM((NK, 4 * BLK * BLK), BF16),
             pltpu.VMEM((NK, 4 * BLK, LANES), BF16),
             pltpu.VMEM((NK, 4 * BLK, LANES), BF16),
-            pltpu.VMEM((512, LANES), F32),
-            pltpu.VMEM((512, LANES), F32),
+            pltpu.VMEM((FOLD, 512, LANES), F32),
+            pltpu.VMEM((FOLD, 512, LANES), F32),
             pltpu.VMEM((4, 3) + block, BF16),
             pltpu.VMEM((8, 16, 2, BLK, LANES), BF16),
-            pltpu.VMEM((2, DEPTH, 2 * LANES), BF16),
+            pltpu.VMEM((2, 4 * LANES, 2 * LANES), BF16),
+            pltpu.VMEM((4, 2, LANES, 2 * LANES), BF16),
             pltpu.VMEM(block, F32),
             pltpu.VMEM((4,) + block, BF16),
             pltpu.VMEM((3,) + block, BF16),
             pltpu.VMEM((4, 8, LANES), jnp.int32),
-            pltpu.VMEM((2, 4 * BLK, 2 * LANES), F32),
+            pltpu.VMEM((4, 2, 4 * BLK, 2 * LANES), F32),
             pltpu.VMEM((NK, NK), jnp.int32),
             pltpu.VMEM((NK, LANES), jnp.int32),
             pltpu.SMEM((NK, LANES), jnp.int32),
@@ -294,8 +332,8 @@
             pltpu.SMEM((4, NA), jnp.int32),
             pltpu.SemaphoreType.DMA((4,)),
             pltpu.SemaphoreType.DMA((6,)),
-            pltpu.SemaphoreType.DMA((11,)),
-            pltpu.SemaphoreType.DMA((11,)),
+            pltpu.SemaphoreType.DMA((22,)),
+            pltpu.SemaphoreType.DMA((22,)),
             pltpu.SemaphoreType.DMA((3,)),
             pltpu.SemaphoreType.DMA((3,)),
         ],

time: 49.3 us -> 46.7 us (0.947)
  Pallas kernels: 47.4 us -> 44.9 us
    pallas_call x1, Pallas kernels: 47.4 us -> 44.9 us  [on_device(): pl.pallas_call(kernel, out_shape=jax.ShapeDtypeStruct(green.shape, F32),...]
where the time goes in v2:
time: 46.7 us; the launch traced here: 46.6 us
  Pallas kernels  44.9 us (96%)
  local copies, waits for them, and re-layouts  1.7 us (4%)
    pallas_call x1, Pallas kernels, on_device(): pl.pallas_call(kernel, out_shape=jax.ShapeDtypeStruct(green.shape, F32),...  44.9 us
    unnamed x1, local copies, waits for them, and re-layouts  1.7 us

profile of v2, /device:TPU:1, one launch (start us, length us, event | category | flops | bytes accessed | tf_op | source)
XLA Modules:
  0.0 46.6 jit_solution(12081953417505464188)
XLA Ops:
  0.0 44.9 %shard_map.73 = f32[2,2,144,128]{3,2,1,0:T(8,128)} custom-call(bf16[2,2,144,128]{3,2,1,0:T(8,128)(2,1)} %green.1, bf16[32,82944]{1,0:T(8,128)(2,1)} %couple.1, s32[32,32]{1,0:T(8,128)} %kdiff.1, s32[32]{0:T(128)} %shift_in.1, f32[32]{0:T(128)} %emit_in.1, f32[32]{0:T(128)} %absorb_in.1, s32[4,16]{1,0:T(4,128)} %bitcast.1), custom_call_target="tpu_custom_call" | custom-call | tf_op jit(solution)/shard_map/pallas_call | solution.py:305
  44.9 1.7 %copy.9 = f32[2,2,144,128]{3,2,1,0:T(8,128)} copy(f32[2,2,144,128]{3,2,1,0:T(8,128)} %shard_map.73) | data formatting | bytes 589824

commit v3 on v2

--- a/solution.py
+++ b/solution.py
@@ -10,7 +10,7 @@
 NA = 16
 NK = 32
 SPAN = 16 * BLK
-FOLD = 3
+FOLD = 6
 MESH = pl.DeviceIdType.MESH
 BF16 = jnp.bfloat16
 F32 = jnp.float32
@@ -74,8 +74,8 @@
 
 
 def kernel(
-    green, couple, kdiff, shift_in, emit_in, absorb_in, nbr_in, out,
-    own, cbuf, cmain, ctail, head, tail, got, tab, rhs, ends, mine, sendbuf, recvbuf, lanes_from, proj,
+    green, couple, kdiff, shift_in, emit_in, absorb_in, nbr_in, mine_out, recvbuf,
+    own, cbuf, cmain, ctail, head, tail, got, tab, rhs, ends, mine, sendbuf, lanes_from, proj,
     kd, invv, inv, shift, emit, absorb, nbr,
     csem, lsem, gs, gr, rs, rr,
 ):
@@ -87,6 +87,9 @@
     across = (kz + 2 - 4 * h, en)
     later = (kz, (en + 1) % count)
     earlier = (kz, (en + count - 1) % count)
+
+    def order(dd):
+        return (2 + 3 * dd + 3 * (dd // 2) + 2 * (dd // 3)) % 4
 
     def column(d):
         return ((kz + 4 * d) % 16, en)
@@ -151,8 +154,7 @@
     for j in range(4):
         lanes_from[j] = sources(nbr, j)
 
-    def table(rho, ir):
-        i, r = ir // 2, ir % 2
+    def table(rho, i, r):
         here = own[i, r] if rho == 0 else got[rho, 1, i, r]
         before, after = got[rho, 0, i, r], got[rho, 2, i, r]
         before = jnp.where(en > 0, before, jnp.zeros_like(before))
@@ -160,32 +162,38 @@
         shift_tables(tab.at[2 * rho + i, :, r], before, here, after)
 
     def tables(rho):
-        @pl.loop(0, 4)
-        def _(ir):
-            table(rho, ir)
+        @pl.loop(0, 2)
+        def _(i):
+            for r in range(2):
+                table(rho, i, r)
 
     fine = lax.broadcasted_iota(jnp.int32, (LANES, LANES), 1) % 16
     spread = jnp.where(lax.broadcasted_iota(jnp.int32, (LANES, LANES), 0) == fine, 1.0, 0.0).astype(BF16)
 
-    def relay(first, last):
-        for j in range(4):
-            if first <= j * 36 // (4 * FOLD) < last:
+    @pl.loop(0, BLK * 4 // 16 // FOLD)
+    def _(part):
+        for j, at in enumerate((0, 0, 3, 4)):
+            @pl.when(part == at)
+            def _():
                 fetch(j).wait()
 
-        @pl.loop(first, last)
-        def _(part):
-            relay_couple(cbuf, cmain, ctail, head, tail, spread, part)
-
-    relay(0, 4)
-    forward(0, (4, 5, 6), 0)
-    relay(4, 6)
-    forward(1, (7,), 0)
-    forward(2, (8,), 0)
-    forward(0, (4, 5, 6), 1)
-    relay(6, 8)
-    forward(1, (7,), 1)
-    forward(2, (8,), 1)
-    relay(8, 12)
+        relay_couple(cbuf, cmain, ctail, head, tail, spread, part)
+
+        @pl.when(part == 1)
+        def _():
+            forward(0, (4, 5, 6), 0)
+
+        @pl.when(part == 2)
+        def _():
+            forward(1, (7,), 0)
+            forward(2, (8,), 0)
+            forward(0, (4, 5, 6), 1)
+
+        @pl.when(part == 3)
+        def _():
+            forward(1, (7,), 1)
+            forward(2, (8,), 1)
+
     forward(4, (9,), 0)
     forward(5, (10,), 0)
     tables(0)
@@ -208,11 +216,11 @@
         return pltpu.make_async_remote_copy(
             src_ref=sendbuf.at[dd], dst_ref=recvbuf.at[dd],
             send_sem=rs.at[dd], recv_sem=rr.at[dd],
-            device_id=column(dd + 1), device_id_type=MESH,
+            device_id=column(order(dd)), device_id_type=MESH,
         )
 
     def phonons_of(dd, kk):
-        k = 8 * ((x + dd + 1) % 4) + 2 * g + kk
+        k = 8 * ((x + order(dd % 4)) % 4) + 2 * g + kk
         return [inv[k, place] for place in places]
 
     def prepare(dd, kk, half):
@@ -259,7 +267,7 @@
     def _(dd):
         prepare(dd, 1, 0)
         project(dd, 0, 0)
-        table(2, dd)
+        table(2, dd // 2, dd % 2)
         prepare(dd + 1, 0, 0)
         project(dd, 1, 0)
 
@@ -283,30 +291,26 @@
         ring(dd - 1).start()
 
     gather(3)
+    keep = pltpu.make_async_copy(mine, mine_out, lsem.at[1])
+    keep.start()
     for pair in hops:
         for piece in pair:
             piece.wait_send()
     for dd in range(3):
+        ring(dd).wait_send()
+    keep.wait()
+    for dd in range(3):
         ring(dd).wait_recv()
-    for kk in range(2):
-        for r in range(2):
-            out[kk, r] = mine[kk, r] + (
-                recvbuf[0, kk, r].astype(F32)
-                + recvbuf[1, kk, r].astype(F32)
-                + recvbuf[2, kk, r].astype(F32)
-            )
-    for dd in range(3):
-        ring(dd).wait_send()
 
 
 def on_device(green, coupling, kdiff, shift, emit_weight, absorb_weight, neighbours):
     hbm = pl.BlockSpec(memory_space=pl.ANY)
     block = (2, 2, BLK, LANES)
-    return pl.pallas_call(
+    total, parts = pl.pallas_call(
         kernel,
-        out_shape=jax.ShapeDtypeStruct(green.shape, F32),
+        out_shape=(jax.ShapeDtypeStruct(block, F32), jax.ShapeDtypeStruct((3,) + block, BF16)),
         in_specs=[hbm] * 7,
-        out_specs=pl.BlockSpec(memory_space=pltpu.VMEM),
+        out_specs=(hbm, hbm),
         scratch_shapes=[
             pltpu.VMEM(block, BF16),
             pltpu.VMEM((NK, 4 * BLK * BLK), BF16),
@@ -320,7 +324,6 @@
             pltpu.VMEM((4, 2, LANES, 2 * LANES), BF16),
             pltpu.VMEM(block, F32),
             pltpu.VMEM((4,) + block, BF16),
-            pltpu.VMEM((3,) + block, BF16),
             pltpu.VMEM((4, 8, LANES), jnp.int32),
             pltpu.VMEM((4, 2, 4 * BLK, 2 * LANES), F32),
             pltpu.VMEM((NK, NK), jnp.int32),
@@ -341,6 +344,7 @@
             collective_id=0, has_side_effects=True, vmem_limit_bytes=62 * 2**20
         ),
     )(green, coupling, kdiff, shift, emit_weight, absorb_weight, neighbours.T)
+    return total + (parts[0].astype(F32) + parts[1].astype(F32) + parts[2].astype(F32))
 
 
 def solution(mesh):

time: 46.7 us -> 46.1 us (0.987)
  other arithmetic: 0 us -> 1.92 us
  local copies, waits for them, and re-layouts: 1.7 us -> 0 us
  Pallas kernels: 44.9 us -> 44.1 us
    add x0 -> x1, other arithmetic: none -> 1.92 us  [on_device(): total + (parts[0].astype(F32) + parts[1].astype(F32) + parts[2].astype(F32))]
    unnamed x1 -> x0, local copies, waits for them, and re-layouts: 1.7 us -> none
    pallas_call x1, Pallas kernels: 44.9 us -> 44.1 us  [on_device(): pl.pallas_call(kernel, out_shape=(jax.ShapeDtypeStruct(block, F32), jax.S...]
where the time goes in v3:
time: 46.1 us; the launch traced here: 46 us
  Pallas kernels  44.1 us (96%)
  other arithmetic  1.92 us (4%)
    pallas_call x1, Pallas kernels, on_device(): pl.pallas_call(kernel, out_shape=(jax.ShapeDtypeStruct(block, F32), jax.S...  44.1 us
    add x1, other arithmetic, on_device(): total + (parts[0].astype(F32) + parts[1].astype(F32) + parts[2].astype(F32))  1.92 us

profile of v3, /device:TPU:1, one launch (start us, length us, event | category | flops | bytes accessed | tf_op | source)
XLA Modules:
  0.0 46.0 jit_solution(13812864920833811997)
XLA Ops:
  0.0 44.1 %shard_map.73 = (f32[2,2,144,128]{3,2,1,0:T(8,128)}, bf16[3,2,2,144,128]{4,3,2,1,0:T(8,128)(2,1)}) custom-call(bf16[2,2,144,128]{3,2,1,0:T(8,128)(2,1)} %green.1, bf16[32,82944]{1,0:T(8,128)(2,1)} %couple.1, s32[32,32]{1,0:T(8,128)} %kdiff.1, s32[32]{0:T(128)} %shift_in.1, f32[32]{0:T(128)} %emit_in.1, f32[32]{0:T(128)} %absorb_in.1, s32[4,16]{1,0:T(4,128)} %bitcast.3), custom_call_target="tpu_custom_call" | custom-call | tf_op jit(solution)/shard_map/pallas_call | solution.py:309
  44.1 1.9 %bitcast_add_fusion = f32[2,2,144,128]{3,2,1,0:T(8,128)} fusion(f32[2,2,144,128]{3,2,1,0:T(8,128)} %get-tuple-element.7, bf16[3,2,2,144,128]{4,3,2,1,0:T(8,128)(2,1)} %get-tuple-element.8), kind=kLoop, calls=%fused_computation | loop fusion | flops 442368 | bytes 1032192 | tf_op jit(solution)/shard_map/add | solution.py:347

commit v4 on v3

--- a/solution.py
+++ b/solution.py
@@ -187,10 +187,10 @@
         def _():
             forward(1, (7,), 0)
             forward(2, (8,), 0)
-            forward(0, (4, 5, 6), 1)
 
         @pl.when(part == 3)
         def _():
+            forward(0, (4, 5, 6), 1)
             forward(1, (7,), 1)
             forward(2, (8,), 1)
 
@@ -212,10 +212,10 @@
             places.append(2 * owner + i)
     group = lax.broadcasted_iota(jnp.int32, (4 * BLK, LANES), 1) // 16
 
-    def ring(dd):
+    def ring(dd, kk):
         return pltpu.make_async_remote_copy(
-            src_ref=sendbuf.at[dd], dst_ref=recvbuf.at[dd],
-            send_sem=rs.at[dd], recv_sem=rr.at[dd],
+            src_ref=sendbuf.at[dd, kk], dst_ref=recvbuf.at[dd, kk],
+            send_sem=rs.at[dd, kk], recv_sem=rr.at[dd, kk],
             device_id=column(order(dd)), device_id_type=MESH,
         )
 
@@ -249,17 +249,16 @@
         part = part + jnp.dot(last, ends[dd, kk], preferred_element_type=F32)
         proj[dd, kk] = proj[dd, kk] + part
 
-    def gather(dd):
-        for kk in range(2):
-            for r in range(2):
-                for m in range(0, BLK, 8):
-                    total = None
-                    for j in range(4):
-                        piece = proj[dd, kk, j * BLK + m : j * BLK + m + 8, r * LANES : (r + 1) * LANES]
-                        piece = jnp.take_along_axis(piece, lanes_from[j], axis=1, mode="promise_in_bounds")
-                        total = piece if total is None else total + piece
-                    mine[kk, r, m : m + 8] = total
-                sendbuf[dd, kk, r] = mine[kk, r].astype(BF16)
+    def gather(dd, kk):
+        for r in range(2):
+            for m in range(0, BLK, 8):
+                total = None
+                for j in range(4):
+                    piece = proj[dd, kk, j * BLK + m : j * BLK + m + 8, r * LANES : (r + 1) * LANES]
+                    piece = jnp.take_along_axis(piece, lanes_from[j], axis=1, mode="promise_in_bounds")
+                    total = piece if total is None else total + piece
+                mine[kk, r, m : m + 8] = total
+            sendbuf[dd, kk, r] = mine[kk, r].astype(BF16)
 
     prepare(0, 0, 0)
 
@@ -278,29 +277,40 @@
     prepare(0, 0, 1)
     prepare(0, 1, 1)
     project(0, 0, 1)
+    gather(0, 0)
+    project(0, 1, 1)
     prepare(1, 0, 1)
-    project(0, 1, 1)
-
-    @pl.loop(1, 4)
+    ring(0, 0).start()
+    gather(0, 1)
+    prepare(1, 1, 1)
+    project(1, 0, 1)
+    prepare(2, 0, 1)
+    project(1, 1, 1)
+    ring(0, 1).start()
+
+    @pl.loop(2, 4)
     def _(dd):
-        gather(dd - 1)
+        gather(dd - 1, 0)
+        gather(dd - 1, 1)
         prepare(dd, 1, 1)
         project(dd, 0, 1)
         prepare(dd + 1, 0, 1)
         project(dd, 1, 1)
-        ring(dd - 1).start()
-
-    gather(3)
+        ring(dd - 1, 0).start()
+        ring(dd - 1, 1).start()
+
+    gather(3, 0)
+    gather(3, 1)
     keep = pltpu.make_async_copy(mine, mine_out, lsem.at[1])
     keep.start()
     for pair in hops:
         for piece in pair:
             piece.wait_send()
-    for dd in range(3):
-        ring(dd).wait_send()
     keep.wait()
     for dd in range(3):
-        ring(dd).wait_recv()
+        for kk in range(2):
+            ring(dd, kk).wait_send()
+            ring(dd, kk).wait_recv()
 
 
 def on_device(green, coupling, kdiff, shift, emit_weight, absorb_weight, neighbours):
@@ -337,8 +347,8 @@
             pltpu.SemaphoreType.DMA((6,)),
             pltpu.SemaphoreType.DMA((22,)),
             pltpu.SemaphoreType.DMA((22,)),
-            pltpu.SemaphoreType.DMA((3,)),
-            pltpu.SemaphoreType.DMA((3,)),
+            pltpu.SemaphoreType.DMA((3, 2)),
+            pltpu.SemaphoreType.DMA((3, 2)),
         ],
         compiler_params=pltpu.CompilerParams(
             collective_id=0, has_side_effects=True, vmem_limit_bytes=62 * 2**20

time: 46.1 us -> 44.8 us (0.972)
  the two profiles are of different devices: /device:TPU:1 before, /device:TPU:6 now
where the time goes in v4:
time: 44.8 us; the launch traced here: 44.7 us
  Pallas kernels  42.7 us (95%)
  other arithmetic  1.92 us (4%)
    pallas_call x1, Pallas kernels, on_device(): pl.pallas_call(kernel, out_shape=(jax.ShapeDtypeStruct(block, F32), jax.S...  42.7 us
    add x1, other arithmetic, on_device(): total + (parts[0].astype(F32) + parts[1].astype(F32) + parts[2].astype(F32))  1.92 us

profile of v4, /device:TPU:6, one launch (start us, length us, event | category | flops | bytes accessed | tf_op | source)
XLA Modules:
  0.0 44.7 jit_solution(8900506456021062141)
XLA Ops:
  0.0 42.7 %shard_map.73 = (f32[2,2,144,128]{3,2,1,0:T(8,128)}, bf16[3,2,2,144,128]{4,3,2,1,0:T(8,128)(2,1)}) custom-call(bf16[2,2,144,128]{3,2,1,0:T(8,128)(2,1)} %green.1, bf16[32,82944]{1,0:T(8,128)(2,1)} %couple.1, s32[32,32]{1,0:T(8,128)} %kdiff.1, s32[32]{0:T(128)} %shift_in.1, f32[32]{0:T(128)} %emit_in.1, f32[32]{0:T(128)} %absorb_in.1, s32[4,16]{1,0:T(4,128)} %bitcast.3), custom_call_target="tpu_custom_call" | custom-call | tf_op jit(solution)/shard_map/pallas_call | solution.py:319
  42.7 1.9 %bitcast_add_fusion = f32[2,2,144,128]{3,2,1,0:T(8,128)} fusion(f32[2,2,144,128]{3,2,1,0:T(8,128)} %get-tuple-element.7, bf16[3,2,2,144,128]{4,3,2,1,0:T(8,128)(2,1)} %get-tuple-element.8), kind=kLoop, calls=%fused_computation | loop fusion | flops 442368 | bytes 1032192 | tf_op jit(solution)/shard_map/add | solution.py:357

commit v5 on v4

--- a/solution.py
+++ b/solution.py
@@ -262,18 +262,22 @@
 
     prepare(0, 0, 0)
 
-    @pl.loop(0, 4)
-    def _(dd):
-        prepare(dd, 1, 0)
-        project(dd, 0, 0)
-        table(2, dd // 2, dd % 2)
-        prepare(dd + 1, 0, 0)
-        project(dd, 1, 0)
-
-    for n in (6, 9, 10):
-        for i in range(2):
-            forward(n, (), i)
-    tables(3)
+    for rho in (2, 3):
+
+        @pl.loop(2 * rho - 4, 2 * rho - 2)
+        def _(dd):
+            prepare(dd, 1, 0)
+            project(dd, 0, 0)
+            for r in range(2):
+                table(rho, dd % 2, r)
+            prepare(dd + 1, 0, 0)
+            project(dd, 1, 0)
+
+        if rho == 2:
+            for n in (6, 9, 10):
+                for i in range(2):
+                    forward(n, (), i)
+
     prepare(0, 0, 1)
     prepare(0, 1, 1)
     project(0, 0, 1)

time: 44.8 us -> 44.1 us (0.984)
  the two profiles are of different devices: /device:TPU:6 before, /device:TPU:1 now
where the time goes in v5:
time: 44.1 us; the launch traced here: 43.7 us
  Pallas kernels  41.7 us (95%)
  other arithmetic  1.92 us (4%)
    pallas_call x1, Pallas kernels, on_device(): pl.pallas_call(kernel, out_shape=(jax.ShapeDtypeStruct(block, F32), jax.S...  41.7 us
    add x1, other arithmetic, on_device(): total + (parts[0].astype(F32) + parts[1].astype(F32) + parts[2].astype(F32))  1.92 us

profile of v5, /device:TPU:1, one launch (start us, length us, event | category | flops | bytes accessed | tf_op | source)
XLA Modules:
  0.0 43.7 jit_solution(4420365993856943408)
XLA Ops:
  0.0 41.7 %shard_map.73 = (f32[2,2,144,128]{3,2,1,0:T(8,128)}, bf16[3,2,2,144,128]{4,3,2,1,0:T(8,128)(2,1)}) custom-call(bf16[2,2,144,128]{3,2,1,0:T(8,128)(2,1)} %green.1, bf16[32,82944]{1,0:T(8,128)(2,1)} %couple.1, s32[32,32]{1,0:T(8,128)} %kdiff.1, s32[32]{0:T(128)} %shift_in.1, f32[32]{0:T(128)} %emit_in.1, f32[32]{0:T(128)} %absorb_in.1, s32[4,16]{1,0:T(4,128)} %bitcast.3), custom_call_target="tpu_custom_call" | custom-call | tf_op jit(solution)/shard_map/pallas_call | solution.py:323
  41.8 1.9 %bitcast_add_fusion = f32[2,2,144,128]{3,2,1,0:T(8,128)} fusion(f32[2,2,144,128]{3,2,1,0:T(8,128)} %get-tuple-element.7, bf16[3,2,2,144,128]{4,3,2,1,0:T(8,128)(2,1)} %get-tuple-element.8), kind=kLoop, calls=%fused_computation | loop fusion | flops 442368 | bytes 1032192 | tf_op jit(solution)/shard_map/add | solution.py:361
